TPU v7x, 32 devices: a whole 2x2x4 slice. The times are simulated.
32 devices in a mesh: dp: 4 (over y, x), ctx: 4 (over z), head: 2 (over core).
Axes of the slice: x: 2, y: 2, z: 4, core: 2. Of those that a mesh axis runs over, the one named last changes fastest.
Arguments:
- inputs: bfloat16 [4, 512, 2048], P('dp', 'ctx', 'head'), may hold values from -1.5 to 1.5
- dt_raw: float32 [4, 512, 32], P('dp', 'ctx', 'head'), may hold values from -4 to 4
- dt_bias: float32 [32], P('head'), may hold values from -1 to 1
- a_log: float32 [32], P('head'), may hold values from -30 to -2.8
- b_in: bfloat16 [4, 512, 128], P('dp', 'ctx'), may hold values from -0.13183594 to 0.13183594
- c_in: bfloat16 [4, 512, 128], P('dp', 'ctx'), may hold values from -0.13183594 to 0.13183594
- skip_gain: float32 [32], P('head'), may hold values from 0.5 to 1.5
- grad_out: bfloat16 [4, 512, 2048], P('dp', 'ctx', 'head'), may hold values from -1.5 to 1.5
- doc_lengths: int32 [4, 4], P('dp'), may hold values from 1 to 256, 512 in all within a row
Outputs:
- grad_inputs: bfloat16 [4, 512, 2048], P('dp', 'ctx', 'head')
- grad_dt_raw: float32 [4, 512, 32], P('dp', 'ctx', 'head')
- grad_b: float32 [4, 512, 128], P('dp', 'ctx')
- grad_c: float32 [4, 512, 128], P('dp', 'ctx')
- grad_a_log: float32 [32], P('head')
- grad_dt_bias: float32 [32], P('head')
- grad_skip: float32 [32], P('head')
Inputs may be any that keep to these rules, and one draw needn't show every extreme that they name: `doc_lengths`: each row lists 4 document lengths laid end to end from the sequence's first position; they sum to 512, and the longest is exactly half of 512.
All inputs are finite; a program needn't handle non-finite values.
Results may differ from a plain program's by a relative error of at most 0.007.
Values sent between devices are 32-bit elements; how exact they have to be, the bound alone decides.
No kernel may reach another device: no remote copies, remote signals or barrier semaphores. Data moves between devices by JAX's collectives and lax.ppermute only.
A program may use at most 64 MiB of HBM per device.

v0:
```python
import jax
import jax.numpy as jnp
from jax import lax
from jax.sharding import PartitionSpec as P

SPAN = 128


def from_behind(array, axis, by):
    count = lax.axis_size(axis)
    pairs = [(i, i + by) for i in range(count) if 0 <= i + by < count]
    return lax.ppermute(array, axis, pairs)


def reverse_cumsum(values, along_axis):
    return jnp.flip(jnp.cumsum(jnp.flip(values, along_axis), axis=along_axis), along_axis)


def doc_index(positions, starts):
    return jnp.sum((starts[None, :] <= positions[:, None]).astype(jnp.int32), axis=1)


def vector_factors(decay_block, segment_block, previous_block):
    cumulative = jnp.cumsum(decay_block, axis=0)
    last_segment = segment_block[-1]
    mask_in = (segment_block == previous_block).astype(jnp.float32)
    mask_out = (segment_block == last_segment).astype(jnp.float32)
    factor_in = mask_in[:, None] * jnp.exp(cumulative)
    factor_out = mask_out[:, None] * jnp.exp(cumulative[-1][None, :] - cumulative)
    span_total = (last_segment == previous_block).astype(jnp.float32) * jnp.exp(cumulative[-1])
    return (cumulative, mask_in, mask_out, factor_in, factor_out, span_total)


def pair_factor(cumulative, segment_block):
    local_pos = jnp.arange(segment_block.shape[0], dtype=jnp.int32)
    allowed = (local_pos[:, None] >= local_pos[None, :]) & (
        segment_block[:, None] == segment_block[None, :]
    )
    spread = cumulative.T[:, :, None] - cumulative.T[:, None, :]
    return jnp.where(allowed[None], jnp.exp(jnp.where(allowed[None], spread, 0.0)), 0.0)


def first_pass(
    inputs_block,
    grads_block,
    b_block,
    c_block,
    step_block,
    decay_block,
    segment_block,
    previous_block,
):
    cumulative, mask_in, mask_out, factor_in, factor_out, span_total = vector_factors(
        decay_block, segment_block, previous_block
    )
    scaled_in = (inputs_block * (factor_out * step_block)[:, :, None]).astype(jnp.bfloat16)
    scaled_grad = (grads_block * factor_in[:, :, None]).astype(jnp.bfloat16)
    state_part = jnp.einsum("shp,sn->hpn", scaled_in, b_block, preferred_element_type=jnp.float32)
    grad_part = jnp.einsum("uhp,un->hpn", scaled_grad, c_block, preferred_element_type=jnp.float32)
    return (span_total, state_part, grad_part)


def span_grads(
    inputs_block,
    grads_block,
    b_block,
    c_block,
    step_block,
    decay_block,
    segment_block,
    previous_block,
    preact_block,
    state_in,
    state_grad,
    decay_rate,
    skip_gain,
):
    cumulative, mask_in, mask_out, factor_in, factor_out, span_total = vector_factors(
        decay_block, segment_block, previous_block
    )
    pair_decay = pair_factor(cumulative, segment_block)
    scores = jnp.einsum("un,sn->us", c_block, b_block, preferred_element_type=jnp.float32)
    cross_term = jnp.einsum(
        "uhp,shp->hus", grads_block, inputs_block, preferred_element_type=jnp.float32
    )
    masked = (pair_decay * scores[None]).astype(jnp.bfloat16)
    weighted = pair_decay * cross_term * step_block.T[:, None, :]
    summed = jnp.sum(weighted, axis=0).astype(jnp.bfloat16)
    products = weighted * scores[None]
    change = jnp.sum(products, axis=2) - jnp.sum(products, axis=1)
    first_term = reverse_cumsum(change, 1).T
    h_low = state_in.astype(jnp.bfloat16)
    e_low = state_grad.astype(jnp.bfloat16)
    along_b = jnp.einsum("tn,hpn->thp", b_block, e_low, preferred_element_type=jnp.float32)
    grad_b_prod = (
        jnp.einsum("hut,uhp->thp", masked, grads_block, preferred_element_type=jnp.float32)
        + factor_out[:, :, None] * along_b
    )
    grad_x = (step_block[:, :, None] * grad_b_prod + skip_gain[None, :, None] * grads_block).astype(
        jnp.bfloat16
    )
    x_state = jnp.einsum("thp,hpn->thn", inputs_block, e_low, preferred_element_type=jnp.float32)
    y_state = jnp.einsum("uhp,hpn->uhn", grads_block, h_low, preferred_element_type=jnp.float32)
    grad_b = jnp.einsum("us,un->sn", summed, c_block, preferred_element_type=jnp.float32) + jnp.sum(
        (step_block * factor_out)[:, :, None] * x_state, axis=1
    )
    grad_c = jnp.einsum("us,sn->un", summed, b_block, preferred_element_type=jnp.float32) + jnp.sum(
        factor_in[:, :, None] * y_state, axis=1
    )
    z_term = jnp.sum(y_state * c_block[:, None, :], axis=2)
    w_term = step_block * jnp.sum(x_state * b_block[:, None, :], axis=2)
    second_term = mask_in[:, None] * reverse_cumsum(factor_in * z_term, 0)
    carried = factor_out * w_term
    third_term = mask_out[:, None] * (jnp.cumsum(carried, axis=0) - carried)
    fourth_term = factor_out * factor_in * jnp.sum(state_grad * state_in, axis=(1, 2))[None, :]
    decay_grad = first_term + second_term + third_term + fourth_term
    x_dot_g = jnp.sum(inputs_block * grad_b_prod, axis=2)
    grad_dt = (x_dot_g + decay_rate[None, :] * decay_grad) * jax.nn.sigmoid(preact_block)
    grad_alog = jnp.sum(decay_grad * step_block, axis=0) * decay_rate
    grad_bias = jnp.sum(grad_dt, axis=0)
    grad_skip = jnp.einsum(
        "thp,thp->h", grads_block, inputs_block, preferred_element_type=jnp.float32
    )
    return (grad_x, grad_dt, grad_b, grad_c, grad_alog, grad_bias, grad_skip)


def local_link(running, pieces):
    decay_gain, held_state = running
    span_total, span_part = pieces
    return ((decay_gain * span_total, span_total[:, None, None] * held_state + span_part), running)


def link_maps(earlier, later):
    return (earlier[0] * later[0], later[0][:, None, None] * earlier[1] + later[1])


def doubling(element, reverse):
    axis_count = lax.axis_size("ctx")
    own_index = lax.axis_index("ctx")
    distances = [1] + [2**power for power in range((axis_count - 1).bit_length())]
    running = element
    for section_num, distance in enumerate(distances):
        shift_by = -distance if reverse else distance
        received = from_behind((running[0], running[1]), "ctx", shift_by)
        source = own_index - shift_by
        present = (source >= 0) & (source < axis_count)
        fixed = (jnp.where(present, received[0], 1.0), received[1])
        if section_num == 0:
            running = fixed
        else:
            running = link_maps(fixed, running)
    return running


def local(inputs, dt_raw, dt_bias, a_log, b_in, c_in, skip_gain, grad_out, doc_lengths):
    token_count = inputs.shape[1]
    head_count = dt_bias.shape[0]
    head_width = inputs.shape[2] // head_count
    state_size = b_in.shape[2]
    span_count = token_count // SPAN
    preact = dt_raw[0] + dt_bias[None, :]
    step_size = jax.nn.softplus(preact)
    decay_rate = -jnp.exp(a_log)
    log_decay = step_size * decay_rate[None, :]
    lengths = doc_lengths[0]
    starts = jnp.cumsum(lengths) - lengths
    positions = lax.axis_index("ctx") * token_count + jnp.arange(token_count, dtype=jnp.int32)
    segment = doc_index(positions, starts)
    previous = doc_index(positions[::SPAN] - 1, starts)
    shaped = (
        inputs[0].reshape(span_count, SPAN, head_count, head_width),
        grad_out[0].reshape(span_count, SPAN, head_count, head_width),
        b_in[0].reshape(span_count, SPAN, state_size),
        c_in[0].reshape(span_count, SPAN, state_size),
        step_size.reshape(span_count, SPAN, head_count),
        log_decay.reshape(span_count, SPAN, head_count),
        segment.reshape(span_count, SPAN),
        previous,
    )
    totals, state_parts, grad_parts = jax.vmap(first_pass)(*shaped)
    start_maps = (
        jnp.ones((head_count,), jnp.float32),
        jnp.zeros((head_count, head_width, state_size), jnp.float32),
    )
    forward_map, (gain_before, local_entry) = lax.scan(
        local_link, start_maps, (totals, state_parts)
    )
    backward_map, (gain_after, local_leave) = lax.scan(
        local_link, start_maps, (totals, grad_parts), reverse=True
    )
    entry_state = doubling(forward_map, False)[1]
    leave_state = doubling(backward_map, True)[1]
    entering = gain_before[:, :, None, None] * entry_state[None] + local_entry
    leaving = gain_after[:, :, None, None] * leave_state[None] + local_leave
    mapped = jax.vmap(span_grads, in_axes=(0, 0, 0, 0, 0, 0, 0, 0, 0, 0, 0, None, None))
    grad_x, grad_dt, grad_b, grad_c, grad_alog, grad_bias, grad_skip = mapped(
        *shaped,
        preact.reshape(span_count, SPAN, head_count),
        entering,
        leaving,
        decay_rate,
        skip_gain
    )
    b_total, c_total = lax.psum(
        (grad_b.reshape(token_count, state_size), grad_c.reshape(token_count, state_size)), "head"
    )
    alog_total, bias_total, skip_total = lax.psum(
        (jnp.sum(grad_alog, axis=0), jnp.sum(grad_bias, axis=0), jnp.sum(grad_skip, axis=0)),
        ("dp", "ctx"),
    )
    return (
        grad_x.reshape(1, token_count, head_count * head_width),
        grad_dt,
        b_total[None],
        c_total[None],
        alog_total,
        bias_total,
        skip_total,
    )


def solution(mesh):
    placed = (
        P("dp", "ctx", "head"),
        P("dp", "ctx", "head"),
        P("head"),
        P("head"),
        P("dp", "ctx", None),
        P("dp", "ctx", None),
        P("head"),
        P("dp", "ctx", "head"),
        P("dp", None),
    )
    return jax.shard_map(
        local,
        mesh=mesh,
        in_specs=placed,
        out_specs=(
            P("dp", "ctx", "head"),
            P("dp", "ctx", "head"),
            P("dp", "ctx", None),
            P("dp", "ctx", None),
            P("head"),
            P("head"),
            P("head"),
        ),
        check_vma=False,
    )
```

profile of v0, /device:TPU:0, one launch (start us, length us, event | category | flops | bytes accessed | tf_op | source)
XLA Modules:
  0.0 140.7 jit_solution(209060816925791621)
XLA Ops:
  7.3 0.8 reduce-window_clone.1
  8.1 1.3 fusion.37
  9.5 0.6 slice.13
  10.1 0.8 copy.101
  10.9 0.7 exponential_negate_fusion
  12.8 0.7 broadcast_multiply_fusion
  13.5 0.2 reduce_window_sum.44
  13.7 1.3 collective-permute-start
  15.0 5.6 %collective-permute-start.5 = (f32[16]{0:T(128)S(1)}, f32[16]{0:T(128)S(1)}, u32[]{:S(2)}, u32[]{:S(2)}) collective-permute-start(f32[16]{0:T(128)S(1)} %get-tuple-element.102), channel_id=1, source_target_pairs={{0,2},{2,4},{4,6},{1,3},{3,5},{5,7},{8,10},{10,12},{12,14},{9,11},... | collective-permute-start | bytes 200 | tf_op jit(solution)/shard_map/ppermute | solution.py:12
  20.7 1.3 compare_convert_fusion
  22.3 0.7 copy-done.1
  23.0 0.2 convolution_add_fusion.1
  23.3 1.4 %collective-permute-start.2 = (f32[16,64,128]{2,1,0:T(8,128)S(1)}, f32[16,64,128]{2,1,0:T(8,128)S(1)}, u32[]{:S(2)}, u32[]{:S(2)}) collective-permute-start(f32[16,64,128]{2,1,0:T(8,128)S(1)} %convolution_add_fusion.1), channel_id=1, source_target_pairs={{2,0},{4,2},{6,4},{3,1},{5,3},{7,5},{10,8},{12,10},{14,12},{11,9},... | collective-permute-start | bytes 1572872 | tf_op jit(solution)/shard_map/ppermute | solution.py:12
  24.8 0.2 copy.107
  25.1 0.7 copy-done
  25.8 0.2 convolution_add_fusion
  26.0 4.6 %collective-permute-start.7 = (f32[16,64,128]{2,1,0:T(8,128)S(1)}, f32[16,64,128]{2,1,0:T(8,128)S(1)}, u32[]{:S(2)}, u32[]{:S(2)}) collective-permute-start(f32[16,64,128]{2,1,0:T(8,128)S(1)} %convolution_add_fusion), channel_id=1, source_target_pairs={{0,2},{2,4},{4,6},{1,3},{3,5},{5,7},{8,10},{10,12},{12,14},{9,11},... | collective-permute-start | bytes 1572872 | tf_op jit(solution)/shard_map/ppermute | solution.py:12
  30.9 0.6 copy-done.5
  31.6 0.9 multiply_reduce_fusion.4
  32.6 6.1 %collective-permute-done.2 = f32[16,64,128]{2,1,0:T(8,128)S(1)} collective-permute-done((f32[16,64,128]{2,1,0:T(8,128)S(1)}, f32[16,64,128]{2,1,0:T(8,128)S(1)}, u32[]{:S(2)}, u32[]{:S(2)}) %collective-permute-start.2) | collective-permute-done | bytes 524320 | tf_op jit(solution)/shard_map/ppermute | solution.py:12
  38.7 1.3 collective-permute-start.3
  40.0 0.5 convolution_bitcast_fusion.2
  40.8 0.3 reduce_window_sum.46
  41.2 4.6 %collective-permute-start.8 = (f32[16,64,128]{2,1,0:T(8,128)S(1)}, f32[16,64,128]{2,1,0:T(8,128)S(1)}, u32[]{:S(2)}, u32[]{:S(2)}) collective-permute-start(f32[16,64,128]{2,1,0:T(8,128)S(1)} %collective-permute-done.7), channel_id=1, source_target_pairs={{0,2},{2,4},{4,6},{1,3},{3,5},{5,7},{8,10},{10,12},{12,14},{9,11},... | collective-permute-start | bytes 1572872 | tf_op jit(solution)/shard_map/ppermute | solution.py:12
  45.8 7.3 %collective-permute-done.3 = f32[16,64,128]{2,1,0:T(8,128)} collective-permute-done((f32[16,64,128]{2,1,0:T(8,128)S(1)}, f32[16,64,128]{2,1,0:T(8,128)}, u32[]{:S(2)}, u32[]{:S(2)}) %collective-permute-start.3) | collective-permute-done | bytes 524320 | tf_op jit(solution)/shard_map/ppermute | solution.py:12
  53.2 1.2 multiply_add_fusion.3
  54.3 1.3 collective-permute-start.4
  55.8 5.5 %collective-permute-start.9 = (f32[16,64,128]{2,1,0:T(8,128)S(1)}, f32[16,64,128]{2,1,0:T(8,128)S(1)}, u32[]{:S(2)}, u32[]{:S(2)}) collective-permute-start(f32[16,64,128]{2,1,0:T(8,128)S(1)} %multiply_add_fusion.1), channel_id=1, source_target_pairs={{0,4},{2,6},{1,5},{3,7},{8,12},{10,14},{9,13},{11,15},{16,20},{18,... | collective-permute-start | bytes 1572872 | tf_op jit(solution)/shard_map/ppermute | solution.py:12
  61.3 0.2 fusion.6
  61.5 3.9 %collective-permute-start.6 = (f32[16]{0:T(128)S(1)}, f32[16]{0:T(128)S(1)}, u32[]{:S(2)}, u32[]{:S(2)}) collective-permute-start(f32[16]{0:T(128)S(1)} %broadcast_select_fusion.1), channel_id=1, source_target_pairs={{0,2},{2,4},{4,6},{1,3},{3,5},{5,7},{8,10},{10,12},{12,14},{9,11},... | collective-permute-start | bytes 200 | tf_op jit(solution)/shard_map/ppermute | solution.py:12
  65.4 1.3 collective-permute-start.1
  66.7 3.5 %collective-permute-done.6 = f32[16]{0:T(128)S(1)} collective-permute-done((f32[16]{0:T(128)S(1)}, f32[16]{0:T(128)S(1)}, u32[]{:S(2)}, u32[]{:S(2)}) %collective-permute-start.6) | collective-permute-done | bytes 96 | tf_op jit(solution)/shard_map/ppermute | solution.py:12
  70.2 0.7 collective-permute-done.1
  70.9 9.1 %collective-permute-done.4 = f32[16,64,128]{2,1,0:T(8,128)S(1)} collective-permute-done((f32[16,64,128]{2,1,0:T(8,128)S(1)}, f32[16,64,128]{2,1,0:T(8,128)S(1)}, u32[]{:S(2)}, u32[]{:S(2)}) %collective-permute-start.4) | collective-permute-done | bytes 524320 | tf_op jit(solution)/shard_map/ppermute | solution.py:12
  80.0 0.3 multiply_reduce_fusion.6
  80.4 0.4 multiply_reduce_fusion.1
  80.8 0.7 multiply_reduce_fusion
  81.8 0.2 reduce_window_sum.47
  82.1 0.7 copy-done.7
  82.8 0.3 multiply_reduce_fusion.7
  83.6 0.8 fusion.4
  84.4 0.8 fusion.5
  85.2 0.7 copy.121
  85.9 0.8 copy.120
  86.7 0.6 copy-done.8
  87.4 44.3 %all-reduce = (f32[16]{0:T(128)}, f32[16]{0:T(128)}, f32[16]{0:T(128)}) all-reduce(f32[16]{0:T(128)S(1)} %fusion.39, f32[16]{0:T(128)S(1)} %get-tuple-element.96, f32[16]{0:T(128)S(1)} %fusion.6), channel_id=1, replica_groups=mesh['dp'=4,'ctx'=4,'head'=2] {'dp','ctx'}, use_global_device_ids=true, to_apply=%region_19.20 | all-reduce | flops 48 | bytes 384 | tf_op jit(solution)/shard_map/psum | solution.py:207
  131.7 1.5 %copy.134 = f32[1,128,128]{2,1,0:T(8,128)} copy(f32[1,128,128]{2,1,0:T(8,128)} %get-tuple-element.119) | data formatting | bytes 131072
  133.2 0.6 copy.135
  (62 shorter events, 2.7 us)
Async XLA Ops:
  7.2 14.8 %copy-start.2 = (bf16[1,128,1024]{2,1,0:T(8,128)(2,1)S(1)}, bf16[1,128,1024]{2,1,0:T(8,128)(2,1)}, u32[]{:S(2)}) copy-start(bf16[1,128,1024]{2,1,0:T(8,128)(2,1)} %param.16) | copy-start | bytes 786436
  7.2 124.5 %all-reduce.4.cloned.1.call-start = ((), (), s32[]{:S(2)}) async-start(), calls=%async_computation | async-start | bytes 262144 | tf_op jit(solution)/shard_map/psum | solution.py:204
  13.7 32.1 %collective-permute-start = (f32[16]{0:T(128)S(1)}, f32[16]{0:T(128)S(1)}, u32[]{:S(2)}, u32[]{:S(2)}) collective-permute-start(f32[16]{0:T(128)S(1)} %get-tuple-element.102), channel_id=1, source_target_pairs={{2,0},{4,2},{6,4},{3,1},{5,3},{7,5},{10,8},{12,10},{14,12},{11,9},... | collective-permute-start | bytes 200 | tf_op jit(solution)/shard_map/ppermute | solution.py:12
  15.0 30.8 %collective-permute-start.5 = (f32[16]{0:T(128)S(1)}, f32[16]{0:T(128)S(1)}, u32[]{:S(2)}, u32[]{:S(2)}) collective-permute-start(f32[16]{0:T(128)S(1)} %get-tuple-element.102), channel_id=1, source_target_pairs={{0,2},{2,4},{4,6},{1,3},{3,5},{5,7},{8,10},{10,12},{12,14},{9,11},... | collective-permute-start | bytes 200 | tf_op jit(solution)/shard_map/ppermute | solution.py:12
  22.3 0.8 copy-start.1
  23.0 1.7 %copy-start.6 = (f32[16]{0:T(128)S(1)}, f32[16]{0:T(128)}, u32[]{:S(2)}) copy-start(f32[16]{0:T(128)} %param.11) | copy-start | bytes 196
  23.2 1.6 %copy-start.3 = (bf16[1,128,1024]{2,1,0:T(8,128)(2,1)S(1)}, bf16[1,128,1024]{2,1,0:T(8,128)(2,1)}, u32[]{:S(2)}) copy-start(bf16[1,128,1024]{2,1,0:T(8,128)(2,1)} %param.9) | copy-start | bytes 786436
  23.3 15.4 %collective-permute-start.2 = (f32[16,64,128]{2,1,0:T(8,128)S(1)}, f32[16,64,128]{2,1,0:T(8,128)S(1)}, u32[]{:S(2)}, u32[]{:S(2)}) collective-permute-start(f32[16,64,128]{2,1,0:T(8,128)S(1)} %convolution_add_fusion.1), channel_id=1, source_target_pairs={{2,0},{4,2},{6,4},{3,1},{5,3},{7,5},{10,8},{12,10},{14,12},{11,9},... | collective-permute-start | bytes 1572872 | tf_op jit(solution)/shard_map/ppermute | solution.py:12
  25.0 0.8 copy-start
  26.0 15.2 %collective-permute-start.7 = (f32[16,64,128]{2,1,0:T(8,128)S(1)}, f32[16,64,128]{2,1,0:T(8,128)S(1)}, u32[]{:S(2)}, u32[]{:S(2)}) collective-permute-start(f32[16,64,128]{2,1,0:T(8,128)S(1)} %convolution_add_fusion), channel_id=1, source_target_pairs={{0,2},{2,4},{4,6},{1,3},{3,5},{5,7},{8,10},{10,12},{12,14},{9,11},... | collective-permute-start | bytes 1572872 | tf_op jit(solution)/shard_map/ppermute | solution.py:12
  30.7 0.7 copy-start.5
  38.7 14.5 %collective-permute-start.3 = (f32[16,64,128]{2,1,0:T(8,128)S(1)}, f32[16,64,128]{2,1,0:T(8,128)}, u32[]{:S(2)}, u32[]{:S(2)}) collective-permute-start(f32[16,64,128]{2,1,0:T(8,128)S(1)} %collective-permute-done.2), channel_id=1, source_target_pairs={{2,0},{4,2},{6,4},{3,1},{5,3},{7,5},{10,8},{12,10},{14,12},{11,9},... | collective-permute-start | bytes 1572872 | tf_op jit(solution)/shard_map/ppermute | solution.py:12
  41.2 14.4 %collective-permute-start.8 = (f32[16,64,128]{2,1,0:T(8,128)S(1)}, f32[16,64,128]{2,1,0:T(8,128)S(1)}, u32[]{:S(2)}, u32[]{:S(2)}) collective-permute-start(f32[16,64,128]{2,1,0:T(8,128)S(1)} %collective-permute-done.7), channel_id=1, source_target_pairs={{0,2},{2,4},{4,6},{1,3},{3,5},{5,7},{8,10},{10,12},{12,14},{9,11},... | collective-permute-start | bytes 1572872 | tf_op jit(solution)/shard_map/ppermute | solution.py:12
  54.3 25.7 %collective-permute-start.4 = (f32[16,64,128]{2,1,0:T(8,128)S(1)}, f32[16,64,128]{2,1,0:T(8,128)S(1)}, u32[]{:S(2)}, u32[]{:S(2)}) collective-permute-start(f32[16,64,128]{2,1,0:T(8,128)S(1)} %multiply_add_fusion.3), channel_id=1, source_target_pairs={{4,0},{6,2},{5,1},{7,3},{12,8},{14,10},{13,9},{15,11},{20,16},{22,... | collective-permute-start | bytes 1572872 | tf_op jit(solution)/shard_map/ppermute | solution.py:12
  55.8 24.3 %collective-permute-start.9 = (f32[16,64,128]{2,1,0:T(8,128)S(1)}, f32[16,64,128]{2,1,0:T(8,128)S(1)}, u32[]{:S(2)}, u32[]{:S(2)}) collective-permute-start(f32[16,64,128]{2,1,0:T(8,128)S(1)} %multiply_add_fusion.1), channel_id=1, source_target_pairs={{0,4},{2,6},{1,5},{3,7},{8,12},{10,14},{9,13},{11,15},{16,20},{18,... | collective-permute-start | bytes 1572872 | tf_op jit(solution)/shard_map/ppermute | solution.py:12
  61.5 8.7 %collective-permute-start.6 = (f32[16]{0:T(128)S(1)}, f32[16]{0:T(128)S(1)}, u32[]{:S(2)}, u32[]{:S(2)}) collective-permute-start(f32[16]{0:T(128)S(1)} %broadcast_select_fusion.1), channel_id=1, source_target_pairs={{0,2},{2,4},{4,6},{1,3},{3,5},{5,7},{8,10},{10,12},{12,14},{9,11},... | collective-permute-start | bytes 200 | tf_op jit(solution)/shard_map/ppermute | solution.py:12
  65.4 5.5 %collective-permute-start.1 = (f32[16]{0:T(128)S(1)}, f32[16]{0:T(128)S(1)}, u32[]{:S(2)}, u32[]{:S(2)}) collective-permute-start(f32[16]{0:T(128)S(1)} %broadcast_select_fusion.3), channel_id=1, source_target_pairs={{2,0},{4,2},{6,4},{3,1},{5,3},{7,5},{10,8},{12,10},{14,12},{11,9},... | collective-permute-start | bytes 200 | tf_op jit(solution)/shard_map/ppermute | solution.py:12
  82.1 0.7 copy-start.7
  86.7 0.7 copy-start.8
  131.7 1.5 %copy-start.4 = (f32[1,128,128]{2,1,0:T(8,128)S(1)}, f32[1,128,128]{2,1,0:T(8,128)}, u32[]{:S(2)}) copy-start(f32[1,128,128]{2,1,0:T(8,128)} %get-tuple-element.120) | copy-start | bytes 196612
Sparse Core Ops, SparseCore 0:
  86.9 20.8 all-reduce.3
where the time goes:
time: 141 us
  blocking collectives  44.3 us (31%)
  starting transfers between devices  30.8 us (22%)
  waiting for transfers between devices  26.8 us (19%)
  between operations  15.8 us (11%)
  local copies, waits for them, and re-layouts  9.75 us (7%)
  other arithmetic  8.3 us (6%)
  matrix products  4.97 us (4%)
    psum x1, blocking collectives, local(): lax.psum((jnp.sum(grad_alog, axis=0), jnp.sum(grad_bias, axis=0), jnp.sum...  44.3 us
    ppermute x10, starting transfers between devices, from_behind(): return lax.ppermute(array, axis, pairs)  30.8 us
    ppermute x10, waiting for transfers between devices, from_behind(): return lax.ppermute(array, axis, pairs)  26.8 us
    unnamed x25, local copies, waits for them, and re-layouts  8.06 us
  transfers between devices with their start and end apart: 11, of which 5 were waited for; matrix products, arithmetic and copies ran while one was open for 5% of the time, Pallas kernels for 0%

commit v1 on v0

--- a/solution.py
+++ b/solution.py
@@ -205,8 +205,11 @@
         (grad_b.reshape(token_count, state_size), grad_c.reshape(token_count, state_size)), "head"
     )
     alog_total, bias_total, skip_total = lax.psum(
-        (jnp.sum(grad_alog, axis=0), jnp.sum(grad_bias, axis=0), jnp.sum(grad_skip, axis=0)),
-        ("dp", "ctx"),
+        lax.psum(
+            (jnp.sum(grad_alog, axis=0), jnp.sum(grad_bias, axis=0), jnp.sum(grad_skip, axis=0)),
+            "ctx",
+        ),
+        "dp",
     )
     return (
         grad_x.reshape(1, token_count, head_count * head_width),

time: 141 us -> 121 us (0.86)
  blocking collectives: 44.3 us -> 24 us
    psum x1, blocking collectives: 44.3 us -> 14 us  [local(): lax.psum((jnp.sum(grad_alog, axis=0), jnp.sum(grad_bias, axis=0), jnp.sum...]
    psum x0 -> x1, blocking collectives: none -> 10 us  [local(): lax.psum(lax.psum((jnp.sum(grad_alog, axis=0), jnp.sum(grad_bias, axis=0)...]
  transfers between devices with their start and end apart: 11 -> 11, of which waited for: 5 -> 5; matrix products, arithmetic and copies ran while one was open for 5% -> 7% of each run, Pallas kernels for 0% -> 0%
where the time goes in v1:
time: 121 us; the launch traced here: 120 us
  starting transfers between devices  30.8 us (25%)
  waiting for transfers between devices  26.8 us (22%)
  blocking collectives  24 us (20%)
  between operations  15.8 us (13%)
  local copies, waits for them, and re-layouts  9.75 us (8%)
  other arithmetic  8.3 us (7%)
  matrix products  4.97 us (4%)
    ppermute x10, starting transfers between devices, from_behind(): return lax.ppermute(array, axis, pairs)  30.8 us
    ppermute x10, waiting for transfers between devices, from_behind(): return lax.ppermute(array, axis, pairs)  26.8 us
    psum x1, blocking collectives, local(): lax.psum((jnp.sum(grad_alog, axis=0), jnp.sum(grad_bias, axis=0), jnp.sum...  14 us
    psum x1, blocking collectives, local(): lax.psum(lax.psum((jnp.sum(grad_alog, axis=0), jnp.sum(grad_bias, axis=0)...  10 us
    unnamed x25, local copies, waits for them, and re-layouts  8.06 us
  transfers between devices with their start and end apart: 11, of which 5 were waited for; matrix products, arithmetic and copies ran while one was open for 7% of the time, Pallas kernels for 0%

profile of v1, /device:TPU:0, one launch (start us, length us, event | category | flops | bytes accessed | tf_op | source)
XLA Modules:
  0.0 120.3 jit_solution(14409676458601922094)
XLA Ops:
  7.3 0.8 reduce-window_clone.1
  8.1 1.3 %fusion.37 = (s32[]{:T(128)}, s32[4]{0:T(128)S(1)}) fusion(s32[]{:T(128)} %bitcast.18, s32[1,4]{1,0:T(1,128)S(1)} %reduce-window_clone.1, s32[1,4]{1,0:T(1,128)} %param.17), kind=kLoop, calls=%fused_computation.89 | loop fusion | flops 15 | bytes 56 | tf_op jit(solution)/shard_map/reduce_sum | solution.py:20
  9.5 0.6 slice.13
  10.1 0.8 copy.101
  10.9 0.7 exponential_negate_fusion
  12.8 0.7 broadcast_multiply_fusion
  13.7 1.3 %collective-permute-start = (f32[16]{0:T(128)S(1)}, f32[16]{0:T(128)S(1)}, u32[]{:S(2)}, u32[]{:S(2)}) collective-permute-start(f32[16]{0:T(128)S(1)} %get-tuple-element.105), channel_id=1, source_target_pairs={{2,0},{4,2},{6,4},{3,1},{5,3},{7,5},{10,8},{12,10},{14,12},{11,9},... | collective-permute-start | bytes 200 | tf_op jit(solution)/shard_map/ppermute | solution.py:12
  15.0 5.6 %collective-permute-start.5 = (f32[16]{0:T(128)S(1)}, f32[16]{0:T(128)S(1)}, u32[]{:S(2)}, u32[]{:S(2)}) collective-permute-start(f32[16]{0:T(128)S(1)} %get-tuple-element.105), channel_id=1, source_target_pairs={{0,2},{2,4},{4,6},{1,3},{3,5},{5,7},{8,10},{10,12},{12,14},{9,11},... | collective-permute-start | bytes 200 | tf_op jit(solution)/shard_map/ppermute | solution.py:12
  20.7 1.3 %compare_convert_fusion = (f32[128]{0:T(128)S(1)}, f32[128]{0:T(128)S(1)}) fusion(s32[128]{0:T(128)S(1)} %convert_reduce_fusion, s32[]{:T(128)} %get-tuple-element.114, s32[]{:T(128)} %bitcast.14), kind=kLoop, calls=%fused_computation.80 | loop fusion | flops 512 | bytes 1544 | tf_op jit(solution)/shard_map/vmap()/convert_element_type | solution.py:26
  22.3 0.7 copy-done.1
  23.0 0.2 convolution_add_fusion.1
  23.3 1.4 %collective-permute-start.2 = (f32[16,64,128]{2,1,0:T(8,128)S(1)}, f32[16,64,128]{2,1,0:T(8,128)S(1)}, u32[]{:S(2)}, u32[]{:S(2)}) collective-permute-start(f32[16,64,128]{2,1,0:T(8,128)S(1)} %convolution_add_fusion.1), channel_id=1, source_target_pairs={{2,0},{4,2},{6,4},{3,1},{5,3},{7,5},{10,8},{12,10},{14,12},{11,9},... | collective-permute-start | bytes 1572872 | tf_op jit(solution)/shard_map/ppermute | solution.py:12
  24.8 0.2 copy.107
  25.1 0.7 copy-done
  25.8 0.2 convolution_add_fusion
  26.0 4.6 %collective-permute-start.7 = (f32[16,64,128]{2,1,0:T(8,128)S(1)}, f32[16,64,128]{2,1,0:T(8,128)S(1)}, u32[]{:S(2)}, u32[]{:S(2)}) collective-permute-start(f32[16,64,128]{2,1,0:T(8,128)S(1)} %convolution_add_fusion), channel_id=1, source_target_pairs={{0,2},{2,4},{4,6},{1,3},{3,5},{5,7},{8,10},{10,12},{12,14},{9,11},... | collective-permute-start | bytes 1572872 | tf_op jit(solution)/shard_map/ppermute | solution.py:12
  30.9 0.6 copy-done.5
  31.6 0.9 multiply_reduce_fusion.4
  32.6 6.1 %collective-permute-done.2 = f32[16,64,128]{2,1,0:T(8,128)S(1)} collective-permute-done((f32[16,64,128]{2,1,0:T(8,128)S(1)}, f32[16,64,128]{2,1,0:T(8,128)S(1)}, u32[]{:S(2)}, u32[]{:S(2)}) %collective-permute-start.2) | collective-permute-done | bytes 524320 | tf_op jit(solution)/shard_map/ppermute | solution.py:12
  38.7 1.3 %collective-permute-start.3 = (f32[16,64,128]{2,1,0:T(8,128)S(1)}, f32[16,64,128]{2,1,0:T(8,128)}, u32[]{:S(2)}, u32[]{:S(2)}) collective-permute-start(f32[16,64,128]{2,1,0:T(8,128)S(1)} %collective-permute-done.2), channel_id=1, source_target_pairs={{2,0},{4,2},{6,4},{3,1},{5,3},{7,5},{10,8},{12,10},{14,12},{11,9},... | collective-permute-start | bytes 1572872 | tf_op jit(solution)/shard_map/ppermute | solution.py:12
  40.0 0.5 convolution_bitcast_fusion.2
  40.8 0.3 reduce_window_sum.46
  41.2 4.6 %collective-permute-start.8 = (f32[16,64,128]{2,1,0:T(8,128)S(1)}, f32[16,64,128]{2,1,0:T(8,128)S(1)}, u32[]{:S(2)}, u32[]{:S(2)}) collective-permute-start(f32[16,64,128]{2,1,0:T(8,128)S(1)} %collective-permute-done.7), channel_id=1, source_target_pairs={{0,2},{2,4},{4,6},{1,3},{3,5},{5,7},{8,10},{10,12},{12,14},{9,11},... | collective-permute-start | bytes 1572872 | tf_op jit(solution)/shard_map/ppermute | solution.py:12
  45.8 7.3 %collective-permute-done.3 = f32[16,64,128]{2,1,0:T(8,128)} collective-permute-done((f32[16,64,128]{2,1,0:T(8,128)S(1)}, f32[16,64,128]{2,1,0:T(8,128)}, u32[]{:S(2)}, u32[]{:S(2)}) %collective-permute-start.3) | collective-permute-done | bytes 524320 | tf_op jit(solution)/shard_map/ppermute | solution.py:12
  53.2 1.2 multiply_add_fusion.3
  54.3 1.3 %collective-permute-start.4 = (f32[16,64,128]{2,1,0:T(8,128)S(1)}, f32[16,64,128]{2,1,0:T(8,128)S(1)}, u32[]{:S(2)}, u32[]{:S(2)}) collective-permute-start(f32[16,64,128]{2,1,0:T(8,128)S(1)} %multiply_add_fusion.3), channel_id=1, source_target_pairs={{4,0},{6,2},{5,1},{7,3},{12,8},{14,10},{13,9},{15,11},{20,16},{22,... | collective-permute-start | bytes 1572872 | tf_op jit(solution)/shard_map/ppermute | solution.py:12
  55.8 5.5 %collective-permute-start.9 = (f32[16,64,128]{2,1,0:T(8,128)S(1)}, f32[16,64,128]{2,1,0:T(8,128)S(1)}, u32[]{:S(2)}, u32[]{:S(2)}) collective-permute-start(f32[16,64,128]{2,1,0:T(8,128)S(1)} %multiply_add_fusion.1), channel_id=1, source_target_pairs={{0,4},{2,6},{1,5},{3,7},{8,12},{10,14},{9,13},{11,15},{16,20},{18,... | collective-permute-start | bytes 1572872 | tf_op jit(solution)/shard_map/ppermute | solution.py:12
  61.3 0.2 fusion.6
  61.5 3.9 %collective-permute-start.6 = (f32[16]{0:T(128)S(1)}, f32[16]{0:T(128)S(1)}, u32[]{:S(2)}, u32[]{:S(2)}) collective-permute-start(f32[16]{0:T(128)S(1)} %broadcast_select_fusion.1), channel_id=1, source_target_pairs={{0,2},{2,4},{4,6},{1,3},{3,5},{5,7},{8,10},{10,12},{12,14},{9,11},... | collective-permute-start | bytes 200 | tf_op jit(solution)/shard_map/ppermute | solution.py:12
  65.4 1.3 %collective-permute-start.1 = (f32[16]{0:T(128)S(1)}, f32[16]{0:T(128)S(1)}, u32[]{:S(2)}, u32[]{:S(2)}) collective-permute-start(f32[16]{0:T(128)S(1)} %broadcast_select_fusion.3), channel_id=1, source_target_pairs={{2,0},{4,2},{6,4},{3,1},{5,3},{7,5},{10,8},{12,10},{14,12},{11,9},... | collective-permute-start | bytes 200 | tf_op jit(solution)/shard_map/ppermute | solution.py:12
  66.7 3.5 %collective-permute-done.6 = f32[16]{0:T(128)S(1)} collective-permute-done((f32[16]{0:T(128)S(1)}, f32[16]{0:T(128)S(1)}, u32[]{:S(2)}, u32[]{:S(2)}) %collective-permute-start.6) | collective-permute-done | bytes 96 | tf_op jit(solution)/shard_map/ppermute | solution.py:12
  70.2 0.7 collective-permute-done.1
  70.9 9.1 %collective-permute-done.4 = f32[16,64,128]{2,1,0:T(8,128)S(1)} collective-permute-done((f32[16,64,128]{2,1,0:T(8,128)S(1)}, f32[16,64,128]{2,1,0:T(8,128)S(1)}, u32[]{:S(2)}, u32[]{:S(2)}) %collective-permute-start.4) | collective-permute-done | bytes 524320 | tf_op jit(solution)/shard_map/ppermute | solution.py:12
  80.0 0.3 multiply_reduce_fusion.6
  80.4 0.4 multiply_reduce_fusion.1
  80.8 0.7 multiply_reduce_fusion
  81.8 0.2 reduce_window_sum.47
  82.1 0.7 copy-done.7
  82.8 0.3 multiply_reduce_fusion.7
  83.6 0.8 fusion.4
  84.4 0.8 fusion.5
  85.2 0.6 copy-done.8
  85.9 14.0 %all-reduce = (f32[16]{0:T(128)S(1)}, f32[16]{0:T(128)S(1)}, f32[16]{0:T(128)S(1)}) all-reduce(f32[16]{0:T(128)S(1)} %fusion.39, f32[16]{0:T(128)S(1)} %get-tuple-element.99, f32[16]{0:T(128)S(1)} %fusion.6), channel_id=1, replica_groups=mesh['dp'=4,'ctx'=4,'head'=2] {'ctx'}, use_global_device_ids=true, to_apply=%region_19.20 | all-reduce | flops 48 | bytes 384 | tf_op jit(solution)/shard_map/psum | solution.py:208
  99.8 10.0 %all-reduce.1 = (f32[16]{0:T(128)}, f32[16]{0:T(128)}, f32[16]{0:T(128)}) all-reduce(f32[16]{0:T(128)S(1)} %get-tuple-element.91, f32[16]{0:T(128)S(1)} %get-tuple-element.92, f32[16]{0:T(128)S(1)} %get-tuple-element.93), channel_id=1, replica_groups=mesh['dp'=4,'ctx'=4,'head'=2] {'dp'}, use_global_device_ids=true, to_apply=%region_20.21 | all-reduce | flops 48 | bytes 384 | tf_op jit(solution)/shard_map/psum | solution.py:207
  109.8 0.7 copy.121
  110.5 0.8 copy.120
  111.4 1.5 %copy.134 = f32[1,128,128]{2,1,0:T(8,128)} copy(f32[1,128,128]{2,1,0:T(8,128)} %get-tuple-element.122) | data formatting | bytes 131072
  112.9 0.6 copy.135
  (63 shorter events, 2.9 us)
Async XLA Ops:
  7.2 14.8 %copy-start.2 = (bf16[1,128,1024]{2,1,0:T(8,128)(2,1)S(1)}, bf16[1,128,1024]{2,1,0:T(8,128)(2,1)}, u32[]{:S(2)}) copy-start(bf16[1,128,1024]{2,1,0:T(8,128)(2,1)} %param.16) | copy-start | bytes 786436
  7.2 104.2 %all-reduce.5.cloned.1.call-start = ((), (), s32[]{:S(2)}) async-start(), calls=%async_computation | async-start | bytes 262144 | tf_op jit(solution)/shard_map/psum | solution.py:204
  13.7 32.1 %collective-permute-start = (f32[16]{0:T(128)S(1)}, f32[16]{0:T(128)S(1)}, u32[]{:S(2)}, u32[]{:S(2)}) collective-permute-start(f32[16]{0:T(128)S(1)} %get-tuple-element.105), channel_id=1, source_target_pairs={{2,0},{4,2},{6,4},{3,1},{5,3},{7,5},{10,8},{12,10},{14,12},{11,9},... | collective-permute-start | bytes 200 | tf_op jit(solution)/shard_map/ppermute | solution.py:12
  15.0 30.8 %collective-permute-start.5 = (f32[16]{0:T(128)S(1)}, f32[16]{0:T(128)S(1)}, u32[]{:S(2)}, u32[]{:S(2)}) collective-permute-start(f32[16]{0:T(128)S(1)} %get-tuple-element.105), channel_id=1, source_target_pairs={{0,2},{2,4},{4,6},{1,3},{3,5},{5,7},{8,10},{10,12},{12,14},{9,11},... | collective-permute-start | bytes 200 | tf_op jit(solution)/shard_map/ppermute | solution.py:12
  22.3 0.8 copy-start.1
  23.0 1.7 %copy-start.6 = (f32[16]{0:T(128)S(1)}, f32[16]{0:T(128)}, u32[]{:S(2)}) copy-start(f32[16]{0:T(128)} %param.11) | copy-start | bytes 196
  23.2 1.6 %copy-start.3 = (bf16[1,128,1024]{2,1,0:T(8,128)(2,1)S(1)}, bf16[1,128,1024]{2,1,0:T(8,128)(2,1)}, u32[]{:S(2)}) copy-start(bf16[1,128,1024]{2,1,0:T(8,128)(2,1)} %param.9) | copy-start | bytes 786436
  23.3 15.4 %collective-permute-start.2 = (f32[16,64,128]{2,1,0:T(8,128)S(1)}, f32[16,64,128]{2,1,0:T(8,128)S(1)}, u32[]{:S(2)}, u32[]{:S(2)}) collective-permute-start(f32[16,64,128]{2,1,0:T(8,128)S(1)} %convolution_add_fusion.1), channel_id=1, source_target_pairs={{2,0},{4,2},{6,4},{3,1},{5,3},{7,5},{10,8},{12,10},{14,12},{11,9},... | collective-permute-start | bytes 1572872 | tf_op jit(solution)/shard_map/ppermute | solution.py:12
  25.0 0.8 copy-start
  26.0 15.2 %collective-permute-start.7 = (f32[16,64,128]{2,1,0:T(8,128)S(1)}, f32[16,64,128]{2,1,0:T(8,128)S(1)}, u32[]{:S(2)}, u32[]{:S(2)}) collective-permute-start(f32[16,64,128]{2,1,0:T(8,128)S(1)} %convolution_add_fusion), channel_id=1, source_target_pairs={{0,2},{2,4},{4,6},{1,3},{3,5},{5,7},{8,10},{10,12},{12,14},{9,11},... | collective-permute-start | bytes 1572872 | tf_op jit(solution)/shard_map/ppermute | solution.py:12
  30.7 0.7 copy-start.5
  38.7 14.5 %collective-permute-start.3 = (f32[16,64,128]{2,1,0:T(8,128)S(1)}, f32[16,64,128]{2,1,0:T(8,128)}, u32[]{:S(2)}, u32[]{:S(2)}) collective-permute-start(f32[16,64,128]{2,1,0:T(8,128)S(1)} %collective-permute-done.2), channel_id=1, source_target_pairs={{2,0},{4,2},{6,4},{3,1},{5,3},{7,5},{10,8},{12,10},{14,12},{11,9},... | collective-permute-start | bytes 1572872 | tf_op jit(solution)/shard_map/ppermute | solution.py:12
  41.2 14.4 %collective-permute-start.8 = (f32[16,64,128]{2,1,0:T(8,128)S(1)}, f32[16,64,128]{2,1,0:T(8,128)S(1)}, u32[]{:S(2)}, u32[]{:S(2)}) collective-permute-start(f32[16,64,128]{2,1,0:T(8,128)S(1)} %collective-permute-done.7), channel_id=1, source_target_pairs={{0,2},{2,4},{4,6},{1,3},{3,5},{5,7},{8,10},{10,12},{12,14},{9,11},... | collective-permute-start | bytes 1572872 | tf_op jit(solution)/shard_map/ppermute | solution.py:12
  54.3 25.7 %collective-permute-start.4 = (f32[16,64,128]{2,1,0:T(8,128)S(1)}, f32[16,64,128]{2,1,0:T(8,128)S(1)}, u32[]{:S(2)}, u32[]{:S(2)}) collective-permute-start(f32[16,64,128]{2,1,0:T(8,128)S(1)} %multiply_add_fusion.3), channel_id=1, source_target_pairs={{4,0},{6,2},{5,1},{7,3},{12,8},{14,10},{13,9},{15,11},{20,16},{22,... | collective-permute-start | bytes 1572872 | tf_op jit(solution)/shard_map/ppermute | solution.py:12
  55.8 24.3 %collective-permute-start.9 = (f32[16,64,128]{2,1,0:T(8,128)S(1)}, f32[16,64,128]{2,1,0:T(8,128)S(1)}, u32[]{:S(2)}, u32[]{:S(2)}) collective-permute-start(f32[16,64,128]{2,1,0:T(8,128)S(1)} %multiply_add_fusion.1), channel_id=1, source_target_pairs={{0,4},{2,6},{1,5},{3,7},{8,12},{10,14},{9,13},{11,15},{16,20},{18,... | collective-permute-start | bytes 1572872 | tf_op jit(solution)/shard_map/ppermute | solution.py:12
  61.5 8.7 %collective-permute-start.6 = (f32[16]{0:T(128)S(1)}, f32[16]{0:T(128)S(1)}, u32[]{:S(2)}, u32[]{:S(2)}) collective-permute-start(f32[16]{0:T(128)S(1)} %broadcast_select_fusion.1), channel_id=1, source_target_pairs={{0,2},{2,4},{4,6},{1,3},{3,5},{5,7},{8,10},{10,12},{12,14},{9,11},... | collective-permute-start | bytes 200 | tf_op jit(solution)/shard_map/ppermute | solution.py:12
  65.4 5.5 %collective-permute-start.1 = (f32[16]{0:T(128)S(1)}, f32[16]{0:T(128)S(1)}, u32[]{:S(2)}, u32[]{:S(2)}) collective-permute-start(f32[16]{0:T(128)S(1)} %broadcast_select_fusion.3), channel_id=1, source_target_pairs={{2,0},{4,2},{6,4},{3,1},{5,3},{7,5},{10,8},{12,10},{14,12},{11,9},... | collective-permute-start | bytes 200 | tf_op jit(solution)/shard_map/ppermute | solution.py:12
  82.1 0.7 copy-start.7
  85.2 0.7 copy-start.8
  111.4 1.5 %copy-start.4 = (f32[1,128,128]{2,1,0:T(8,128)S(1)}, f32[1,128,128]{2,1,0:T(8,128)}, u32[]{:S(2)}) copy-start(f32[1,128,128]{2,1,0:T(8,128)} %get-tuple-element.123) | copy-start | bytes 196612
Sparse Core Ops, SparseCore 0:
  85.3 20.8 all-reduce.4
